TPU v7x, 256 devices: a whole 4x4x8 slice. The times are simulated.
256 devices in a mesh: fsdp: 32 (over y, x, core), tp: 8 (over z).
Axes of the slice: x: 4, y: 4, z: 8, core: 2. Of those that a mesh axis runs over, the one named last changes fastest.
Arguments:
- learner_flat: bfloat16 [2, 159383552], P(None, ('fsdp', 'tp')), may hold values from -1.796875 to 1.796875
- param_offsets: int32 [2, 128, 4], replicated, may hold values from 0 to 622336, as said below
- owner_map: int32 [2, 128], replicated, may hold values from 0 to 31, as said below
- slice_map: int32 [32, 8], replicated, may hold values from 0 to 7, each once within a row
Outputs:
- query_absorbed: bfloat16 [2, 128, 1536, 512], P(None, 'fsdp', 'tp')
- output_absorbed: bfloat16 [2, 128, 7168, 512], P(None, 'fsdp', 'tp')
Inputs may be any that keep to these rules, and one draw needn't show every extreme that they name: `param_offsets`: in each layer the pieces of all heads' four parameters lie in a rank's 622592 entries one after another in some order, without gaps or intersections; a piece of a parameter holds that parameter's entries divided by 256; the last piece of each layer is a key up-projection piece. `owner_map`: in each layer every index of fsdp owns exactly 4 heads.
All inputs are finite; a program needn't handle non-finite values.
Results may differ from a plain program's by a relative error of at most 0.001.
Values may be sent and summed in bfloat16 or wider, within the bound.
A program may use at most 64 MiB of HBM per device.

v0:
```python
import math
import jax
import jax.numpy as jnp
from jax import lax
from jax.sharding import PartitionSpec as P

D = 7168
QR = 1536
KVR = 512
QK_NOPE = 128
V_DIM = 128


def for_sending(shard):
    return jax.tree.map(lambda a: a.astype(jnp.bfloat16) if a.dtype == jnp.float32 else a, shard)


def head_order(owner_map, per_group):
    head_count = owner_map.shape[1]
    head_index = jnp.arange(head_count, dtype=jnp.int32)
    same_owner = owner_map[:, :, None] == owner_map[:, None, :]
    before = head_index[None, None, :] < head_index[None, :, None]
    head_rank = jnp.sum(jnp.logical_and(same_owner, before).astype(jnp.int32), axis=2)
    head_slot = owner_map * per_group + head_rank
    slot_hits = head_slot[:, :, None] == head_index[None, None, :]
    return jnp.sum(jnp.where(slot_hits, head_index[None, :, None], 0), axis=1)


def cut_pieces(local_flat, begins, width_now, granule):
    layer_count, heads_here = begins.shape
    row_table = local_flat.reshape(layer_count, local_flat.shape[1] // granule, granule)
    row_steps = jnp.arange(width_now // granule, dtype=jnp.int32)
    row_ids = (begins[:, :, None] // granule + row_steps[None, None, :]).reshape(
        layer_count, heads_here * (width_now // granule)
    )
    picked = jnp.take_along_axis(row_table, row_ids[:, :, None], axis=1)
    return picked.reshape(layer_count, heads_here, width_now)


def refresh(local_flat, param_offsets, head_at, slice_row):
    fsdp_ways = lax.axis_size("fsdp")
    tensor_ways = lax.axis_size("tp")
    rank_total = fsdp_ways * tensor_ways
    layer_count = local_flat.shape[0]
    per_group = head_at.shape[1] // fsdp_ways
    widths = (
        QR * QK_NOPE // rank_total,
        QK_NOPE * KVR // rank_total,
        V_DIM * KVR // rank_total,
        D * V_DIM // rank_total,
    )
    granule = math.gcd(math.gcd(widths[0], widths[1]), math.gcd(widths[2], widths[3]))
    begins = jnp.take_along_axis(param_offsets, head_at[:, :, None], axis=1)
    pieces = tuple(
        (
            cut_pieces(local_flat, begins[:, :, kind_id], widths[kind_id], granule).reshape(
                layer_count, fsdp_ways, per_group, 1, widths[kind_id]
            )
            for kind_id in range(4)
        )
    )
    arrived = jax.tree.map(
        lambda part, own: part.astype(own.dtype),
        lax.all_to_all(for_sending(pieces), "fsdp", split_axis=1, concat_axis=3, tiled=True),
        pieces,
    )
    query_part, key_part, value_part, out_part = tuple(
        (
            arrived[kind_id].reshape(layer_count, per_group, fsdp_ways, 1, widths[kind_id])
            for kind_id in range(4)
        )
    )
    slice_query = QR // tensor_ways
    slice_output = D // tensor_ways
    blocks = fsdp_ways // tensor_ways

    def to_send(part_in, width_now):
        grouped = part_in.reshape(layer_count, per_group, tensor_ways, blocks, width_now)
        return jnp.take(grouped, slice_row, axis=2).reshape(
            layer_count, per_group, tensor_ways, blocks, 1, width_now
        )

    query_rows, out_rows = (
        lax.all_to_all(
            to_send(query_part, widths[0]), "tp", split_axis=2, concat_axis=4, tiled=True
        ),
        lax.all_to_all(to_send(out_part, widths[3]), "tp", split_axis=2, concat_axis=4, tiled=True),
    )
    query_rows = query_rows.reshape(layer_count, per_group, slice_query, QK_NOPE)
    out_rows = out_rows.reshape(layer_count, per_group, slice_output, V_DIM)
    key_full, value_full = (
        lax.all_gather(key_part, "tp", axis=3, tiled=True),
        lax.all_gather(value_part, "tp", axis=3, tiled=True),
    )
    key_full = key_full.reshape(layer_count, per_group, QK_NOPE, KVR)
    value_full = value_full.reshape(layer_count, per_group, V_DIM, KVR)
    query_absorbed = jnp.einsum(
        "lhrc,lhck->lhrk", query_rows, key_full, preferred_element_type=jnp.float32
    ).astype(jnp.bfloat16)
    output_absorbed = jnp.einsum(
        "lhrc,lhck->lhrk", out_rows, value_full, preferred_element_type=jnp.float32
    ).astype(jnp.bfloat16)
    return (query_absorbed, output_absorbed)


def per_device(learner_flat, param_offsets, owner_map, slice_map):
    fsdp_ways = lax.axis_size("fsdp")
    per_group = owner_map.shape[1] // fsdp_ways
    head_at = head_order(owner_map, per_group)
    slice_row = lax.dynamic_index_in_dim(slice_map, lax.axis_index("fsdp"), 0, keepdims=False)
    layer_results = [
        refresh(
            learner_flat[layer_id : layer_id + 1],
            param_offsets[layer_id : layer_id + 1],
            head_at[layer_id : layer_id + 1],
            slice_row,
        )
        for layer_id in range(learner_flat.shape[0])
    ]
    query_absorbed = jnp.concatenate([result_pair[0] for result_pair in layer_results], axis=0)
    output_absorbed = jnp.concatenate([result_pair[1] for result_pair in layer_results], axis=0)
    return (query_absorbed, output_absorbed)


def solution(mesh):
    placed = (P(None, ("fsdp", "tp")), P(), P(), P())
    return jax.shard_map(
        per_device,
        mesh=mesh,
        in_specs=placed,
        out_specs=(P(None, "fsdp", "tp", None), P(None, "fsdp", "tp", None)),
        check_vma=False,
    )
```

profile of v0, /device:TPU:38, one launch (start us, length us, event | category | flops | bytes accessed | tf_op | source)
XLA Modules:
  0.0 371.7 jit_solution(2697430013469942218)
XLA Ops:
  4.4 28.8 %slice_reduce_fusion.1 = (bf16[622592]{0:T(1024)(128)(2,1)S(1)}, bf16[622592]{0:T(1024)(128)(2,1)}) fusion(bf16[2,622592]{1,0:T(2,128)(2,1)} %param.16), kind=kLoop, calls=%fused_computation.18 | loop fusion | bytes 4980736 | tf_op jit(solution)/shard_map/slice | solution.py:113
  35.2 7.6 %all-to-all-start.8 = ((bf16[1,32,4,1,256]{4,2,3,0,1:T(4,128)(2,1)}), bf16[1,32,4,1,256]{4,2,3,0,1:T(4,128)(2,1)S(1)}, u32[]{:S(2)}, u32[]{:S(2)}) async-start(bf16[1,32,4,1,256]{4,2,3,0,1:T(4,128)(2,1)} %bitcast.57), calls=%async_computation.8 | async-start | bytes 131072 | tf_op jit(solution)/shard_map/all_to_all | solution.py:64
  46.9 2.1 gather_fusion.1
  48.9 2.2 reshape.662
  55.8 7.4 %all-to-all-start.2 = ((bf16[1,32,4,1,256]{4,2,3,0,1:T(4,128)(2,1)}), bf16[1,32,4,1,256]{4,2,3,0,1:T(4,128)(2,1)S(1)}, u32[]{:S(2)}, u32[]{:S(2)}) async-start(bf16[1,32,4,1,256]{4,2,3,0,1:T(4,128)(2,1)} %bitcast.18), calls=%async_computation.2 | async-start | bytes 131072 | tf_op jit(solution)/shard_map/all_to_all | solution.py:64
  65.1 3.8 %all-to-all-done.2 = bf16[1,32,4,1,256]{4,2,3,0,1:T(4,128)(2,1)S(1)} async-done(((bf16[1,32,4,1,256]{4,2,3,0,1:T(4,128)(2,1)}), bf16[1,32,4,1,256]{4,2,3,0,1:T(4,128)(2,1)S(1)}, u32[]{:S(2)}, u32[]{:S(2)}) %all-to-all-start.2) | async-done | bytes 65568 | tf_op jit(solution)/shard_map/all_to_all | solution.py:64
  68.9 6.2 %all-to-all-start.11 = ((bf16[1,32,4,1,256]{4,2,3,0,1:T(4,128)(2,1)}), bf16[1,32,4,1,256]{4,2,3,0,1:T(4,128)(2,1)}, u32[]{:S(2)}, u32[]{:S(2)}) async-start(bf16[1,32,4,1,256]{4,2,3,0,1:T(4,128)(2,1)} %bitcast.74), calls=%async_computation.11 | async-start | bytes 131072 | tf_op jit(solution)/shard_map/all_to_all | solution.py:64
  75.1 5.5 %gather_fusion.8 = bf16[1792,256]{1,0:T(8,128)(2,1)S(1)} fusion(bf16[2432,256]{1,0:T(8,128)(2,1)S(1)} %reshape.643, s32[2048]{0:T(1024)S(1)} %pad_clamp_fusion.1), kind=kCustom, calls=%fused_computation.4.clone | custom fusion | bytes 1842176 | tf_op jit(solution)/shard_map/jit(take_along_axis)/gather | solution.py:36
  83.8 7.5 %all-to-all-start.5 = ((bf16[1,32,4,1,256]{4,2,3,0,1:T(4,128)(2,1)}), bf16[1,32,4,1,256]{4,2,3,0,1:T(4,128)(2,1)S(1)}, u32[]{:S(2)}, u32[]{:S(2)}) async-start(bf16[1,32,4,1,256]{4,2,3,0,1:T(4,128)(2,1)} %bitcast.40), calls=%async_computation.5 | async-start | bytes 131072 | tf_op jit(solution)/shard_map/all_to_all | solution.py:64
  91.3 2.1 gather_fusion.5
  93.4 3.6 all-to-all-done.5
  97.6 5.6 %all-to-all-start = ((bf16[1,32,4,1,768]{4,2,3,0,1:T(4,128)(2,1)}), bf16[1,32,4,1,768]{4,2,3,0,1:T(4,128)(2,1)S(1)}, u32[]{:S(2)}, u32[]{:S(2)}) async-start(bf16[1,32,4,1,768]{4,2,3,0,1:T(4,128)(2,1)} %bitcast.6), calls=%async_computation | async-start | bytes 393216 | tf_op jit(solution)/shard_map/all_to_all | solution.py:64
  104.1 5.7 %all-to-all-done = bf16[1,32,4,1,768]{4,2,3,0,1:T(4,128)(2,1)S(1)} async-done(((bf16[1,32,4,1,768]{4,2,3,0,1:T(4,128)(2,1)}), bf16[1,32,4,1,768]{4,2,3,0,1:T(4,128)(2,1)S(1)}, u32[]{:S(2)}, u32[]{:S(2)}) %all-to-all-start) | async-done | bytes 196640 | tf_op jit(solution)/shard_map/all_to_all | solution.py:64
  109.8 5.5 %all-to-all-start.3 = ((bf16[1,32,4,1,768]{4,2,3,0,1:T(4,128)(2,1)}), bf16[1,32,4,1,768]{4,2,3,0,1:T(4,128)(2,1)S(1)}, u32[]{:S(2)}, u32[]{:S(2)}) async-start(bf16[1,32,4,1,768]{4,2,3,0,1:T(4,128)(2,1)} %bitcast.28), calls=%async_computation.3 | async-start | bytes 393216 | tf_op jit(solution)/shard_map/all_to_all | solution.py:64
  116.9 4.9 %all-to-all-done.3 = bf16[1,32,4,1,768]{4,2,3,0,1:T(4,128)(2,1)S(1)} async-done(((bf16[1,32,4,1,768]{4,2,3,0,1:T(4,128)(2,1)}), bf16[1,32,4,1,768]{4,2,3,0,1:T(4,128)(2,1)S(1)}, u32[]{:S(2)}, u32[]{:S(2)}) %all-to-all-start.3) | async-done | bytes 196640 | tf_op jit(solution)/shard_map/all_to_all | solution.py:64
  121.9 5.5 %all-to-all-start.6 = ((bf16[1,32,4,1,3584]{4,2,3,0,1:T(4,128)(2,1)}), bf16[1,32,4,1,3584]{4,2,3,0,1:T(4,128)(2,1)S(1)}, u32[]{:S(2)}, u32[]{:S(2)}) async-start(bf16[1,32,4,1,3584]{4,2,3,0,1:T(4,128)(2,1)} %bitcast.45), calls=%async_computation.6 | async-start | bytes 1835008 | tf_op jit(solution)/shard_map/all_to_all | solution.py:64
  127.4 5.5 %gather_fusion.11 = bf16[1792,256]{1,0:T(8,128)(2,1)S(1)} fusion(bf16[2432,256]{1,0:T(8,128)(2,1)S(1)} %reshape.662, s32[2048]{0:T(1024)S(1)} %pad_clamp_fusion), kind=kCustom, calls=%fused_computation.12.clone | custom fusion | bytes 1842176 | tf_op jit(solution)/shard_map/jit(take_along_axis)/gather | solution.py:36
  134.5 6.2 %all-to-all-done.6 = bf16[1,32,4,1,3584]{4,2,3,0,1:T(4,128)(2,1)S(1)} async-done(((bf16[1,32,4,1,3584]{4,2,3,0,1:T(4,128)(2,1)}), bf16[1,32,4,1,3584]{4,2,3,0,1:T(4,128)(2,1)S(1)}, u32[]{:S(2)}, u32[]{:S(2)}) %all-to-all-start.6) | async-done | bytes 917536 | tf_op jit(solution)/shard_map/all_to_all | solution.py:64
  140.7 6.4 %all-to-all-start.9 = ((bf16[1,32,4,1,3584]{4,2,3,0,1:T(4,128)(2,1)}), bf16[1,32,4,1,3584]{4,2,3,0,1:T(4,128)(2,1)S(1)}, u32[]{:S(2)}, u32[]{:S(2)}) async-start(bf16[1,32,4,1,3584]{4,2,3,0,1:T(4,128)(2,1)} %bitcast.62), calls=%async_computation.9 | async-start | bytes 1835008 | tf_op jit(solution)/shard_map/all_to_all | solution.py:64
  149.9 10.5 %all-to-all-done.9 = bf16[1,32,4,1,3584]{4,2,3,0,1:T(4,128)(2,1)S(1)} async-done(((bf16[1,32,4,1,3584]{4,2,3,0,1:T(4,128)(2,1)}), bf16[1,32,4,1,3584]{4,2,3,0,1:T(4,128)(2,1)S(1)}, u32[]{:S(2)}, u32[]{:S(2)}) %all-to-all-start.9) | async-done | bytes 917536 | tf_op jit(solution)/shard_map/all_to_all | solution.py:64
  160.4 8.6 %all-to-all-start.1 = ((bf16[1,4,8,4,1,768]{5,3,1,4,0,2:T(4,128)(2,1)}), bf16[1,4,8,4,1,768]{5,3,1,4,0,2:T(4,128)(2,1)S(1)}, u32[]{:S(2)}, u32[]{:S(2)}) async-start(bf16[1,4,8,4,1,768]{5,3,1,4,0,2:T(4,128)(2,1)} %get-tuple-element.46), calls=%async_computation.1 | async-start | bytes 393216 | tf_op jit(solution)/shard_map/all_to_all | solution.py:84
  172.4 7.0 %all-to-all-done.1 = bf16[1,4,8,4,1,768]{5,3,1,4,0,2:T(4,128)(2,1)S(1)} async-done(((bf16[1,4,8,4,1,768]{5,3,1,4,0,2:T(4,128)(2,1)}), bf16[1,4,8,4,1,768]{5,3,1,4,0,2:T(4,128)(2,1)S(1)}, u32[]{:S(2)}, u32[]{:S(2)}) %all-to-all-start.1) | async-done | bytes 196640 | tf_op jit(solution)/shard_map/all_to_all | solution.py:84
  179.4 4.8 %all-to-all-start.4 = ((bf16[1,4,8,4,1,768]{5,3,1,4,0,2:T(4,128)(2,1)}), bf16[1,4,8,4,1,768]{5,3,1,4,0,2:T(4,128)(2,1)S(1)}, u32[]{:S(2)}, u32[]{:S(2)}) async-start(bf16[1,4,8,4,1,768]{5,3,1,4,0,2:T(4,128)(2,1)} %get-tuple-element.47), calls=%async_computation.4 | async-start | bytes 393216 | tf_op jit(solution)/shard_map/all_to_all | solution.py:84
  186.0 7.8 %all-to-all-done.4 = bf16[1,4,8,4,1,768]{5,3,1,4,0,2:T(4,128)(2,1)S(1)} async-done(((bf16[1,4,8,4,1,768]{5,3,1,4,0,2:T(4,128)(2,1)}), bf16[1,4,8,4,1,768]{5,3,1,4,0,2:T(4,128)(2,1)S(1)}, u32[]{:S(2)}, u32[]{:S(2)}) %all-to-all-start.4) | async-done | bytes 196640 | tf_op jit(solution)/shard_map/all_to_all | solution.py:84
  193.8 27.8 %all_to_all.180 = bf16[1,4,8,4,1,3584]{5,3,1,4,0,2:T(4,128)(2,1)S(1)} all-to-all(bf16[1,4,8,4,1,3584]{5,3,1,4,0,2:T(4,128)(2,1)S(1)} %get-tuple-element.44), channel_id=1, replica_groups=mesh['fsdp'=32,'tp'=8] {'tp'}, dimensions={2} | all-to-all | bytes 1835008 | tf_op jit(solution)/shard_map/all_to_all | solution.py:87
  221.6 4.9 %all-to-all-start.10 = ((bf16[1,4,8,4,1,3584]{5,3,1,4,0,2:T(4,128)(2,1)}), bf16[1,4,8,4,1,3584]{5,3,1,4,0,2:T(4,128)(2,1)S(1)}, u32[]{:S(2)}, u32[]{:S(2)}) async-start(bf16[1,4,8,4,1,3584]{5,3,1,4,0,2:T(4,128)(2,1)} %get-tuple-element.45), calls=%async_computation.10 | async-start | bytes 1835008 | tf_op jit(solution)/shard_map/all_to_all | solution.py:87
  226.5 41.6 %all-gather = bf16[1,1,4,32,8,256]{5,3,4,2,1,0:T(8,128)(2,1)S(1)} all-gather(bf16[1,1,4,32,1,256]{5,3,4,2,1,0:T(8,128)(2,1)S(1)} %bitcast.216), channel_id=2, replica_groups=mesh['fsdp'=32,'tp'=8] {'tp'}, dimensions={4}, use_global_device_ids=true | all-gather | bytes 589824 | tf_op jit(solution)/shard_map/all_gather | solution.py:92
  268.6 25.5 %all-gather.2 = bf16[1,1,4,32,8,256]{5,3,4,2,1,0:T(8,128)(2,1)S(1)} all-gather(bf16[1,1,4,32,1,256]{5,3,4,2,1,0:T(8,128)(2,1)S(1)} %bitcast.217), channel_id=4, replica_groups=mesh['fsdp'=32,'tp'=8] {'tp'}, dimensions={4}, use_global_device_ids=true | all-gather | bytes 589824 | tf_op jit(solution)/shard_map/all_gather | solution.py:93
  294.6 25.5 %all-gather.1 = bf16[1,1,4,32,8,256]{5,3,4,2,1,0:T(8,128)(2,1)S(1)} all-gather(bf16[1,1,4,32,1,256]{5,3,4,2,1,0:T(8,128)(2,1)S(1)} %bitcast.218), channel_id=3, replica_groups=mesh['fsdp'=32,'tp'=8] {'tp'}, dimensions={4}, use_global_device_ids=true | all-gather | bytes 589824 | tf_op jit(solution)/shard_map/all_gather | solution.py:92
  323.3 25.2 %all-gather.3 = bf16[1,1,4,32,8,256]{5,3,4,2,1,0:T(8,128)(2,1)S(1)} all-gather(bf16[1,1,4,32,1,256]{5,3,4,2,1,0:T(8,128)(2,1)S(1)} %bitcast.219), channel_id=5, replica_groups=mesh['fsdp'=32,'tp'=8] {'tp'}, dimensions={4}, use_global_device_ids=true | all-gather | bytes 589824 | tf_op jit(solution)/shard_map/all_gather | solution.py:93
  364.8 2.1 convert_bitcast_fusion
  368.1 3.7 pad_maximum_fusion
  (138 shorter events, 53.7 us)
Async XLA Ops:
  0.6 146.5 %copy-start = (s32[32,8]{0,1:T(8,128)S(1)}, s32[32,8]{0,1:T(8,128)}, u32[]{:S(2)}) copy-start(s32[32,8]{0,1:T(8,128)} %param.19) | copy-start | bytes 3076
  35.2 20.7 %all-to-all-start.8 = ((bf16[1,32,4,1,256]{4,2,3,0,1:T(4,128)(2,1)}), bf16[1,32,4,1,256]{4,2,3,0,1:T(4,128)(2,1)S(1)}, u32[]{:S(2)}, u32[]{:S(2)}) async-start(bf16[1,32,4,1,256]{4,2,3,0,1:T(4,128)(2,1)} %bitcast.57), calls=%async_computation.8 | async-start | bytes 131072 | tf_op jit(solution)/shard_map/all_to_all | solution.py:64
  55.8 13.1 %all-to-all-start.2 = ((bf16[1,32,4,1,256]{4,2,3,0,1:T(4,128)(2,1)}), bf16[1,32,4,1,256]{4,2,3,0,1:T(4,128)(2,1)S(1)}, u32[]{:S(2)}, u32[]{:S(2)}) async-start(bf16[1,32,4,1,256]{4,2,3,0,1:T(4,128)(2,1)} %bitcast.18), calls=%async_computation.2 | async-start | bytes 131072 | tf_op jit(solution)/shard_map/all_to_all | solution.py:64
  68.9 14.9 %all-to-all-start.11 = ((bf16[1,32,4,1,256]{4,2,3,0,1:T(4,128)(2,1)}), bf16[1,32,4,1,256]{4,2,3,0,1:T(4,128)(2,1)}, u32[]{:S(2)}, u32[]{:S(2)}) async-start(bf16[1,32,4,1,256]{4,2,3,0,1:T(4,128)(2,1)} %bitcast.74), calls=%async_computation.11 | async-start | bytes 131072 | tf_op jit(solution)/shard_map/all_to_all | solution.py:64
  80.6 22.6 %copy-start.13 = (pred[384]{0:T(512)(128)(4,1)S(1)}, pred[384]{0:T(512)(128)(4,1)}, u32[]{:S(2)}) copy-start(pred[384]{0:T(512)(128)(4,1)} %get-tuple-element.38) | copy-start | bytes 1156
  83.8 13.2 %all-to-all-start.5 = ((bf16[1,32,4,1,256]{4,2,3,0,1:T(4,128)(2,1)}), bf16[1,32,4,1,256]{4,2,3,0,1:T(4,128)(2,1)S(1)}, u32[]{:S(2)}, u32[]{:S(2)}) async-start(bf16[1,32,4,1,256]{4,2,3,0,1:T(4,128)(2,1)} %bitcast.40), calls=%async_computation.5 | async-start | bytes 131072 | tf_op jit(solution)/shard_map/all_to_all | solution.py:64
  91.3 24.0 %copy-start.12 = (pred[1792]{0:T(1024)(128)(4,1)S(1)}, pred[1792]{0:T(1024)(128)(4,1)}, u32[]{:S(2)}) copy-start(pred[1792]{0:T(1024)(128)(4,1)} %get-tuple-element.16) | copy-start | bytes 5380
  97.0 0.6 copy-start.8
  97.6 12.2 %all-to-all-start = ((bf16[1,32,4,1,768]{4,2,3,0,1:T(4,128)(2,1)}), bf16[1,32,4,1,768]{4,2,3,0,1:T(4,128)(2,1)S(1)}, u32[]{:S(2)}, u32[]{:S(2)}) async-start(bf16[1,32,4,1,768]{4,2,3,0,1:T(4,128)(2,1)} %bitcast.6), calls=%async_computation | async-start | bytes 393216 | tf_op jit(solution)/shard_map/all_to_all | solution.py:64
  109.8 5.5 %copy-start.1 = (bf16[1,32,4,1,768]{4,2,3,0,1:T(4,128)(2,1)}, bf16[1,32,4,1,768]{4,2,3,0,1:T(4,128)(2,1)S(1)}, u32[]{:S(2)}) copy-start(bf16[1,32,4,1,768]{4,2,3,0,1:T(4,128)(2,1)S(1)} %all-to-all-done) | copy-start | bytes 589828
  109.8 12.1 %all-to-all-start.3 = ((bf16[1,32,4,1,768]{4,2,3,0,1:T(4,128)(2,1)}), bf16[1,32,4,1,768]{4,2,3,0,1:T(4,128)(2,1)S(1)}, u32[]{:S(2)}, u32[]{:S(2)}) async-start(bf16[1,32,4,1,768]{4,2,3,0,1:T(4,128)(2,1)} %bitcast.28), calls=%async_computation.3 | async-start | bytes 393216 | tf_op jit(solution)/shard_map/all_to_all | solution.py:64
  115.6 11.7 %copy-start.10 = (s32[1,1792,1]{1,2,0:T(1,128)S(1)}, s32[1,1792,1]{1,2,0:T(1,128)}, u32[]{:S(2)}) copy-start(s32[1,1792,1]{1,2,0:T(1,128)} %get-tuple-element.35) | copy-start | bytes 21508
  121.9 11.0 %copy-start.4 = (bf16[1,32,4,1,768]{4,2,3,0,1:T(4,128)(2,1)}, bf16[1,32,4,1,768]{4,2,3,0,1:T(4,128)(2,1)S(1)}, u32[]{:S(2)}) copy-start(bf16[1,32,4,1,768]{4,2,3,0,1:T(4,128)(2,1)S(1)} %all-to-all-done.3) | copy-start | bytes 589828
  121.9 18.8 %all-to-all-start.6 = ((bf16[1,32,4,1,3584]{4,2,3,0,1:T(4,128)(2,1)}), bf16[1,32,4,1,3584]{4,2,3,0,1:T(4,128)(2,1)S(1)}, u32[]{:S(2)}, u32[]{:S(2)}) async-start(bf16[1,32,4,1,3584]{4,2,3,0,1:T(4,128)(2,1)} %bitcast.45), calls=%async_computation.6 | async-start | bytes 1835008 | tf_op jit(solution)/shard_map/all_to_all | solution.py:64
  127.4 5.5 %copy-start.11 = (pred[1792]{0:T(1024)(128)(4,1)S(1)}, pred[1792]{0:T(1024)(128)(4,1)}, u32[]{:S(2)}) copy-start(pred[1792]{0:T(1024)(128)(4,1)} %get-tuple-element.34) | copy-start | bytes 5380
  133.2 14.1 %copy-start.2 = (bf16[1,32,4,1,768]{4,2,3,0,1:T(4,128)(2,1)S(1)}, bf16[1,32,4,1,768]{4,2,3,0,1:T(4,128)(2,1)}, u32[]{:S(2)}) copy-start(bf16[1,32,4,1,768]{4,2,3,0,1:T(4,128)(2,1)} %copy-done.1) | copy-start | bytes 589828
  134.5 12.9 %copy-start.5 = (bf16[1,32,4,1,768]{4,2,3,0,1:T(4,128)(2,1)S(1)}, bf16[1,32,4,1,768]{4,2,3,0,1:T(4,128)(2,1)}, u32[]{:S(2)}) copy-start(bf16[1,32,4,1,768]{4,2,3,0,1:T(4,128)(2,1)} %copy-done.4) | copy-start | bytes 589828
  140.7 19.8 %all-to-all-start.9 = ((bf16[1,32,4,1,3584]{4,2,3,0,1:T(4,128)(2,1)}), bf16[1,32,4,1,3584]{4,2,3,0,1:T(4,128)(2,1)S(1)}, u32[]{:S(2)}, u32[]{:S(2)}) async-start(bf16[1,32,4,1,3584]{4,2,3,0,1:T(4,128)(2,1)} %bitcast.62), calls=%async_computation.9 | async-start | bytes 1835008 | tf_op jit(solution)/shard_map/all_to_all | solution.py:64
  160.4 19.0 %all-to-all-start.1 = ((bf16[1,4,8,4,1,768]{5,3,1,4,0,2:T(4,128)(2,1)}), bf16[1,4,8,4,1,768]{5,3,1,4,0,2:T(4,128)(2,1)S(1)}, u32[]{:S(2)}, u32[]{:S(2)}) async-start(bf16[1,4,8,4,1,768]{5,3,1,4,0,2:T(4,128)(2,1)} %get-tuple-element.46), calls=%async_computation.1 | async-start | bytes 393216 | tf_op jit(solution)/shard_map/all_to_all | solution.py:84
  179.4 6.6 %copy-start.3 = (bf16[1,4,8,4,1,768]{5,3,1,4,0,2:T(4,128)(2,1)}, bf16[1,4,8,4,1,768]{5,3,1,4,0,2:T(4,128)(2,1)S(1)}, u32[]{:S(2)}) copy-start(bf16[1,4,8,4,1,768]{5,3,1,4,0,2:T(4,128)(2,1)S(1)} %all-to-all-done.1) | copy-start | bytes 589828
  179.4 14.4 %all-to-all-start.4 = ((bf16[1,4,8,4,1,768]{5,3,1,4,0,2:T(4,128)(2,1)}), bf16[1,4,8,4,1,768]{5,3,1,4,0,2:T(4,128)(2,1)S(1)}, u32[]{:S(2)}, u32[]{:S(2)}) async-start(bf16[1,4,8,4,1,768]{5,3,1,4,0,2:T(4,128)(2,1)} %get-tuple-element.47), calls=%async_computation.4 | async-start | bytes 393216 | tf_op jit(solution)/shard_map/all_to_all | solution.py:84
  193.8 27.8 %copy-start.6 = (bf16[1,4,8,4,1,768]{5,3,1,4,0,2:T(4,128)(2,1)}, bf16[1,4,8,4,1,768]{5,3,1,4,0,2:T(4,128)(2,1)S(1)}, u32[]{:S(2)}) copy-start(bf16[1,4,8,4,1,768]{5,3,1,4,0,2:T(4,128)(2,1)S(1)} %all-to-all-done.4) | copy-start | bytes 589828
  221.6 141.6 %all-to-all-start.10 = ((bf16[1,4,8,4,1,3584]{5,3,1,4,0,2:T(4,128)(2,1)}), bf16[1,4,8,4,1,3584]{5,3,1,4,0,2:T(4,128)(2,1)S(1)}, u32[]{:S(2)}, u32[]{:S(2)}) async-start(bf16[1,4,8,4,1,3584]{5,3,1,4,0,2:T(4,128)(2,1)} %get-tuple-element.45), calls=%async_computation.10 | async-start | bytes 1835008 | tf_op jit(solution)/shard_map/all_to_all | solution.py:87
  268.6 26.0 %copy-start.9 = (bf16[1,32,4,1,256]{4,2,3,0,1:T(4,128)(2,1)S(1)}, bf16[1,32,4,1,256]{4,2,3,0,1:T(4,128)(2,1)}, u32[]{:S(2)}) copy-start(bf16[1,32,4,1,256]{4,2,3,0,1:T(4,128)(2,1)} %copy-done.8) | copy-start | bytes 196612
  358.5 1.3 copy-start.7
where the time goes:
time: 373 us; the launch traced here: 372 us
  blocking collectives  146 us (39%)
  local copies, waits for them, and re-layouts  85.3 us (23%)
  starting transfers between devices  69.7 us (19%)
  waiting for transfers between devices  49.5 us (13%)
  other arithmetic  15.4 us (4%)
  matrix products  4.9 us (1%)
    all_gather x2, blocking collectives, refresh(): lax.all_gather(key_part, 'tp', axis=3, tiled=True)  67.1 us
    all_to_all x8, starting transfers between devices, refresh(): lax.all_to_all(for_sending(pieces), 'fsdp', split_axis=1, concat_axis=3,...  51.5 us
    all_gather x2, blocking collectives, refresh(): lax.all_gather(value_part, 'tp', axis=3, tiled=True)  50.7 us
    all_to_all x8, waiting for transfers between devices, refresh(): lax.all_to_all(for_sending(pieces), 'fsdp', split_axis=1, concat_axis=3,...  34.7 us
    slice x1, local copies, waits for them, and re-layouts, per_device(): learner_flat[layer_id:layer_id + 1]  28.8 us
    all_to_all x1, blocking collectives, refresh(): lax.all_to_all(to_send(out_part, widths[3]), 'tp', split_axis=2, concat_a...  27.8 us
    gather x8, local copies, waits for them, and re-layouts, cut_pieces(): picked = jnp.take_along_axis(row_table, row_ids[:, :, None], axis=1)  18.4 us
    all_to_all x2, waiting for transfers between devices, refresh(): lax.all_to_all(to_send(query_part, widths[0]), 'tp', split_axis=2, concat...  14.8 us
  transfers between devices with their start and end apart: 11, of which 8 were waited for; matrix products, arithmetic and copies ran while one was open for 17% of the time, Pallas kernels for 0%

commit v1 on v0

--- a/solution.py
+++ b/solution.py
@@ -1,3 +1,4 @@
+import functools
 import math
 import jax
 import jax.numpy as jnp
@@ -9,6 +10,18 @@
 KVR = 512
 QK_NOPE = 128
 V_DIM = 128
+
+
+def pair_quarters_up(matrix, row_dim):
+    n_slots = lax.axis_size("tp")
+    frames = [n_slots if ii == row_dim else 1 for ii in range(matrix.ndim)]
+    block_last = lax.all_to_all(
+        jnp.tile(matrix, frames), "tp", concat_axis=row_dim, split_axis=row_dim, tiled=True
+    )
+    return block_last
+
+
+answer_rows = functools.partial(pair_quarters_up, row_dim=3)
 
 
 def for_sending(shard):
@@ -90,7 +103,7 @@
     out_rows = out_rows.reshape(layer_count, per_group, slice_output, V_DIM)
     key_full, value_full = (
         lax.all_gather(key_part, "tp", axis=3, tiled=True),
-        lax.all_gather(value_part, "tp", axis=3, tiled=True),
+        answer_rows(value_part),
     )
     key_full = key_full.reshape(layer_count, per_group, QK_NOPE, KVR)
     value_full = value_full.reshape(layer_count, per_group, V_DIM, KVR)

time: 373 us -> 361 us (0.968)
  blocking collectives: 146 us -> 97 us
  waiting for transfers between devices: 49.5 us -> 81.4 us
  starting transfers between devices: 69.7 us -> 79.1 us
  local copies, waits for them, and re-layouts: 85.3 us -> 80 us
    all_gather x2 -> x0, blocking collectives: 50.7 us -> none  [refresh(): lax.all_gather(value_part, 'tp', axis=3, tiled=True)]
    all_to_all x0 -> x2, waiting for transfers between devices: none -> 28.8 us  [pair_quarters_up(): lax.all_to_all(jnp.tile(matrix, frames), 'tp', concat_axis=row_dim, split...]
    all_to_all x0 -> x2, starting transfers between devices: none -> 11.2 us  [pair_quarters_up(): lax.all_to_all(jnp.tile(matrix, frames), 'tp', concat_axis=row_dim, split...]
    all_to_all x8, waiting for transfers between devices: 34.7 us -> 44.2 us  [refresh(): lax.all_to_all(for_sending(pieces), 'fsdp', split_axis=1, concat_axis=3,...]
    all_to_all x2, waiting for transfers between devices: 14.8 us -> 8.47 us  [refresh(): lax.all_to_all(to_send(query_part, widths[0]), 'tp', split_axis=2, concat...]
    another operation x8 -> x12, local copies, waits for them, and re-layouts: 9.43 us -> 8.41 us
  transfers between devices with their start and end apart: 11 -> 13, of which waited for: 8 -> 11; matrix products, arithmetic and copies ran while one was open for 17% -> 15% of each run, Pallas kernels for 0% -> 0%
where the time goes in v1:
time: 361 us; the launch traced here: 358 us
  blocking collectives  97 us (27%)
  waiting for transfers between devices  81.4 us (23%)
  local copies, waits for them, and re-layouts  80 us (22%)
  starting transfers between devices  79.1 us (22%)
  other arithmetic  14.3 us (4%)
  matrix products  4.92 us (1%)
    all_gather x2, blocking collectives, refresh(): lax.all_gather(key_part, 'tp', axis=3, tiled=True)  68 us
    all_to_all x8, starting transfers between devices, refresh(): lax.all_to_all(for_sending(pieces), 'fsdp', split_axis=1, concat_axis=3,...  49.2 us
    all_to_all x8, waiting for transfers between devices, refresh(): lax.all_to_all(for_sending(pieces), 'fsdp', split_axis=1, concat_axis=3,...  44.2 us
    all_to_all x1, blocking collectives, refresh(): lax.all_to_all(to_send(out_part, widths[3]), 'tp', split_axis=2, concat_a...  29 us
    slice x1, local copies, waits for them, and re-layouts, per_device(): learner_flat[layer_id:layer_id + 1]  28.8 us
    all_to_all x2, waiting for transfers between devices, pair_quarters_up(): lax.all_to_all(jnp.tile(matrix, frames), 'tp', concat_axis=row_dim, split...  28.8 us
    gather x8, local copies, waits for them, and re-layouts, cut_pieces(): picked = jnp.take_along_axis(row_table, row_ids[:, :, None], axis=1)  18.4 us
    all_to_all x2, starting transfers between devices, refresh(): lax.all_to_all(to_send(query_part, widths[0]), 'tp', split_axis=2, concat...  13.8 us
  transfers between devices with their start and end apart: 13, of which 11 were waited for; matrix products, arithmetic and copies ran while one was open for 15% of the time, Pallas kernels for 0%

profile of v1, /device:TPU:38, one launch (start us, length us, event | category | flops | bytes accessed | tf_op | source)
XLA Modules:
  0.0 358.0 jit_solution(15795769746665352532)
XLA Ops:
  4.4 28.8 %slice_reduce_fusion.1 = (bf16[622592]{0:T(1024)(128)(2,1)S(1)}, bf16[622592]{0:T(1024)(128)(2,1)}) fusion(bf16[2,622592]{1,0:T(2,128)(2,1)} %param.16), kind=kLoop, calls=%fused_computation.18 | loop fusion | bytes 4980736 | tf_op jit(solution)/shard_map/slice | solution.py:126
  35.2 7.6 %all-to-all-start.8 = ((bf16[1,32,4,1,256]{4,2,3,0,1:T(4,128)(2,1)}), bf16[1,32,4,1,256]{4,2,3,0,1:T(4,128)(2,1)S(1)}, u32[]{:S(2)}, u32[]{:S(2)}) async-start(bf16[1,32,4,1,256]{4,2,3,0,1:T(4,128)(2,1)} %bitcast.57), calls=%async_computation.8 | async-start | bytes 131072 | tf_op jit(solution)/shard_map/all_to_all | solution.py:77
  49.2 2.2 reshape.656
  55.6 7.4 %all-to-all-start.2 = ((bf16[1,32,4,1,256]{4,2,3,0,1:T(4,128)(2,1)}), bf16[1,32,4,1,256]{4,2,3,0,1:T(4,128)(2,1)S(1)}, u32[]{:S(2)}, u32[]{:S(2)}) async-start(bf16[1,32,4,1,256]{4,2,3,0,1:T(4,128)(2,1)} %bitcast.18), calls=%async_computation.2 | async-start | bytes 131072 | tf_op jit(solution)/shard_map/all_to_all | solution.py:77
  66.1 2.6 all-to-all-done.2
  68.7 5.6 %all-to-all-start = ((bf16[1,32,4,1,768]{4,2,3,0,1:T(4,128)(2,1)}), bf16[1,32,4,1,768]{4,2,3,0,1:T(4,128)(2,1)S(1)}, u32[]{:S(2)}, u32[]{:S(2)}) async-start(bf16[1,32,4,1,768]{4,2,3,0,1:T(4,128)(2,1)} %bitcast.6), calls=%async_computation | async-start | bytes 393216 | tf_op jit(solution)/shard_map/all_to_all | solution.py:77
  74.3 6.6 %all-to-all-done = bf16[1,32,4,1,768]{4,2,3,0,1:T(4,128)(2,1)S(1)} async-done(((bf16[1,32,4,1,768]{4,2,3,0,1:T(4,128)(2,1)}), bf16[1,32,4,1,768]{4,2,3,0,1:T(4,128)(2,1)S(1)}, u32[]{:S(2)}, u32[]{:S(2)}) %all-to-all-start) | async-done | bytes 196640 | tf_op jit(solution)/shard_map/all_to_all | solution.py:77
  80.9 5.5 %all-to-all-start.3 = ((bf16[1,32,4,1,768]{4,2,3,0,1:T(4,128)(2,1)}), bf16[1,32,4,1,768]{4,2,3,0,1:T(4,128)(2,1)S(1)}, u32[]{:S(2)}, u32[]{:S(2)}) async-start(bf16[1,32,4,1,768]{4,2,3,0,1:T(4,128)(2,1)} %bitcast.28), calls=%async_computation.3 | async-start | bytes 393216 | tf_op jit(solution)/shard_map/all_to_all | solution.py:77
  86.4 6.6 %all-to-all-done.3 = bf16[1,32,4,1,768]{4,2,3,0,1:T(4,128)(2,1)S(1)} async-done(((bf16[1,32,4,1,768]{4,2,3,0,1:T(4,128)(2,1)}), bf16[1,32,4,1,768]{4,2,3,0,1:T(4,128)(2,1)S(1)}, u32[]{:S(2)}, u32[]{:S(2)}) %all-to-all-start.3) | async-done | bytes 196640 | tf_op jit(solution)/shard_map/all_to_all | solution.py:77
  92.9 5.5 %all-to-all-start.12 = ((bf16[1,32,4,1,256]{4,2,3,0,1:T(4,128)(2,1)}), bf16[1,32,4,1,256]{4,2,3,0,1:T(4,128)(2,1)S(1)}, u32[]{:S(2)}, u32[]{:S(2)}) async-start(bf16[1,32,4,1,256]{4,2,3,0,1:T(4,128)(2,1)} %bitcast.75), calls=%async_computation.12 | async-start | bytes 131072 | tf_op jit(solution)/shard_map/all_to_all | solution.py:77
  100.1 4.1 %all-to-all-done.12 = bf16[1,32,4,1,256]{4,2,3,0,1:T(4,128)(2,1)S(1)} async-done(((bf16[1,32,4,1,256]{4,2,3,0,1:T(4,128)(2,1)}), bf16[1,32,4,1,256]{4,2,3,0,1:T(4,128)(2,1)S(1)}, u32[]{:S(2)}, u32[]{:S(2)}) %all-to-all-start.12) | async-done | bytes 65568 | tf_op jit(solution)/shard_map/all_to_all | solution.py:77
  104.1 5.6 %all-to-all-start.5 = ((bf16[1,32,4,1,256]{4,2,3,0,1:T(4,128)(2,1)}), bf16[1,32,4,1,256]{4,2,3,0,1:T(4,128)(2,1)S(1)}, u32[]{:S(2)}, u32[]{:S(2)}) async-start(bf16[1,32,4,1,256]{4,2,3,0,1:T(4,128)(2,1)} %bitcast.40), calls=%async_computation.5 | async-start | bytes 131072 | tf_op jit(solution)/shard_map/all_to_all | solution.py:77
  110.7 4.8 %all-to-all-done.5 = bf16[1,32,4,1,256]{4,2,3,0,1:T(4,128)(2,1)S(1)} async-done(((bf16[1,32,4,1,256]{4,2,3,0,1:T(4,128)(2,1)}), bf16[1,32,4,1,256]{4,2,3,0,1:T(4,128)(2,1)S(1)}, u32[]{:S(2)}, u32[]{:S(2)}) %all-to-all-start.5) | async-done | bytes 65568 | tf_op jit(solution)/shard_map/all_to_all | solution.py:77
  115.5 8.6 %all-to-all-start.1 = ((bf16[1,4,8,4,1,768]{5,3,1,4,0,2:T(4,128)(2,1)}), bf16[1,4,8,4,1,768]{5,3,1,4,0,2:T(4,128)(2,1)}, u32[]{:S(2)}, u32[]{:S(2)}) async-start(bf16[1,4,8,4,1,768]{5,3,1,4,0,2:T(4,128)(2,1)} %get-tuple-element.46), calls=%async_computation.1 | async-start | bytes 393216 | tf_op jit(solution)/shard_map/all_to_all | solution.py:97
  125.9 5.5 %gather_fusion.8 = bf16[1792,256]{1,0:T(8,128)(2,1)S(1)} fusion(bf16[2432,256]{1,0:T(8,128)(2,1)S(1)} %reshape.637, s32[2048]{0:T(1024)S(1)} %pad_clamp_fusion.1), kind=kCustom, calls=%fused_computation.4.clone | custom fusion | bytes 1842176 | tf_op jit(solution)/shard_map/jit(take_along_axis)/gather | solution.py:49
  133.4 5.2 %all-to-all-start.4 = ((bf16[1,4,8,4,1,768]{5,3,1,4,0,2:T(4,128)(2,1)}), bf16[1,4,8,4,1,768]{5,3,1,4,0,2:T(4,128)(2,1)S(1)}, u32[]{:S(2)}, u32[]{:S(2)}) async-start(bf16[1,4,8,4,1,768]{5,3,1,4,0,2:T(4,128)(2,1)} %get-tuple-element.47), calls=%async_computation.4 | async-start | bytes 393216 | tf_op jit(solution)/shard_map/all_to_all | solution.py:97
  140.9 6.4 %all-to-all-done.4 = bf16[1,4,8,4,1,768]{5,3,1,4,0,2:T(4,128)(2,1)S(1)} async-done(((bf16[1,4,8,4,1,768]{5,3,1,4,0,2:T(4,128)(2,1)}), bf16[1,4,8,4,1,768]{5,3,1,4,0,2:T(4,128)(2,1)S(1)}, u32[]{:S(2)}, u32[]{:S(2)}) %all-to-all-start.4) | async-done | bytes 196640 | tf_op jit(solution)/shard_map/all_to_all | solution.py:97
  147.4 5.6 %all-to-all-start.6 = ((bf16[1,32,4,1,3584]{4,2,3,0,1:T(4,128)(2,1)}), bf16[1,32,4,1,3584]{4,2,3,0,1:T(4,128)(2,1)S(1)}, u32[]{:S(2)}, u32[]{:S(2)}) async-start(bf16[1,32,4,1,3584]{4,2,3,0,1:T(4,128)(2,1)} %bitcast.45), calls=%async_computation.6 | async-start | bytes 1835008 | tf_op jit(solution)/shard_map/all_to_all | solution.py:77
  153.1 5.5 %gather_fusion.11 = bf16[1792,256]{1,0:T(8,128)(2,1)S(1)} fusion(bf16[2432,256]{1,0:T(8,128)(2,1)S(1)} %reshape.656, s32[2048]{0:T(1024)S(1)} %pad_clamp_fusion), kind=kCustom, calls=%fused_computation.12.clone | custom fusion | bytes 1842176 | tf_op jit(solution)/shard_map/jit(take_along_axis)/gather | solution.py:49
  160.2 6.2 %all-to-all-done.6 = bf16[1,32,4,1,3584]{4,2,3,0,1:T(4,128)(2,1)S(1)} async-done(((bf16[1,32,4,1,3584]{4,2,3,0,1:T(4,128)(2,1)}), bf16[1,32,4,1,3584]{4,2,3,0,1:T(4,128)(2,1)S(1)}, u32[]{:S(2)}, u32[]{:S(2)}) %all-to-all-start.6) | async-done | bytes 917536 | tf_op jit(solution)/shard_map/all_to_all | solution.py:77
  166.4 6.5 %all-to-all-start.10 = ((bf16[1,32,4,1,3584]{4,2,3,0,1:T(4,128)(2,1)}), bf16[1,32,4,1,3584]{4,2,3,0,1:T(4,128)(2,1)S(1)}, u32[]{:S(2)}, u32[]{:S(2)}) async-start(bf16[1,32,4,1,3584]{4,2,3,0,1:T(4,128)(2,1)} %bitcast.63), calls=%async_computation.10 | async-start | bytes 1835008 | tf_op jit(solution)/shard_map/all_to_all | solution.py:77
  172.9 13.3 %all-to-all-done.10 = bf16[1,32,4,1,3584]{4,2,3,0,1:T(4,128)(2,1)S(1)} async-done(((bf16[1,32,4,1,3584]{4,2,3,0,1:T(4,128)(2,1)}), bf16[1,32,4,1,3584]{4,2,3,0,1:T(4,128)(2,1)S(1)}, u32[]{:S(2)}, u32[]{:S(2)}) %all-to-all-start.10) | async-done | bytes 917536 | tf_op jit(solution)/shard_map/all_to_all | solution.py:77
  187.1 5.5 %all-to-all-start.9 = ((bf16[1,4,32,8,256]{4,2,1,0,3:T(8,128)(2,1)}), bf16[1,4,32,8,256]{4,2,1,0,3:T(8,128)(2,1)}, u32[]{:S(2)}, u32[]{:S(2)}) async-start(bf16[1,4,32,8,256]{4,2,1,0,3:T(8,128)(2,1)} %tile.17), calls=%async_computation.9 | async-start | bytes 1048576 | tf_op jit(solution)/shard_map/all_to_all | solution.py:18
  196.1 13.8 %all-to-all-done.9 = bf16[1,4,32,8,256]{4,2,1,0,3:T(8,128)(2,1)} async-done(((bf16[1,4,32,8,256]{4,2,1,0,3:T(8,128)(2,1)}), bf16[1,4,32,8,256]{4,2,1,0,3:T(8,128)(2,1)}, u32[]{:S(2)}, u32[]{:S(2)}) %all-to-all-start.9) | async-done | bytes 524320 | tf_op jit(solution)/shard_map/all_to_all | solution.py:18
  210.7 5.8 %all-to-all-start.13 = ((bf16[1,4,32,8,256]{4,2,1,0,3:T(8,128)(2,1)}), bf16[1,4,32,8,256]{4,2,1,0,3:T(8,128)(2,1)}, u32[]{:S(2)}, u32[]{:S(2)}) async-start(bf16[1,4,32,8,256]{4,2,1,0,3:T(8,128)(2,1)} %tile.19), calls=%async_computation.13 | async-start | bytes 1048576 | tf_op jit(solution)/shard_map/all_to_all | solution.py:18
  218.3 14.9 %all-to-all-done.13 = bf16[1,4,32,8,256]{4,2,1,0,3:T(8,128)(2,1)} async-done(((bf16[1,4,32,8,256]{4,2,1,0,3:T(8,128)(2,1)}), bf16[1,4,32,8,256]{4,2,1,0,3:T(8,128)(2,1)}, u32[]{:S(2)}, u32[]{:S(2)}) %all-to-all-start.13) | async-done | bytes 524320 | tf_op jit(solution)/shard_map/all_to_all | solution.py:18
  233.2 29.0 %all_to_all.190 = bf16[1,4,8,4,1,3584]{5,3,1,4,0,2:T(4,128)(2,1)S(1)} all-to-all(bf16[1,4,8,4,1,3584]{5,3,1,4,0,2:T(4,128)(2,1)S(1)} %get-tuple-element.44), channel_id=1, replica_groups=mesh['fsdp'=32,'tp'=8] {'tp'}, dimensions={2} | all-to-all | bytes 1835008 | tf_op jit(solution)/shard_map/all_to_all | solution.py:100
  262.2 4.9 %all-to-all-start.11 = ((bf16[1,4,8,4,1,3584]{5,3,1,4,0,2:T(4,128)(2,1)}), bf16[1,4,8,4,1,3584]{5,3,1,4,0,2:T(4,128)(2,1)S(1)}, u32[]{:S(2)}, u32[]{:S(2)}) async-start(bf16[1,4,8,4,1,3584]{5,3,1,4,0,2:T(4,128)(2,1)} %get-tuple-element.45), calls=%async_computation.11 | async-start | bytes 1835008 | tf_op jit(solution)/shard_map/all_to_all | solution.py:100
  267.1 42.6 %all-gather = bf16[1,1,4,32,8,256]{5,3,4,2,1,0:T(8,128)(2,1)S(1)} all-gather(bf16[1,1,4,32,1,256]{5,3,4,2,1,0:T(8,128)(2,1)S(1)} %bitcast.215), channel_id=2, replica_groups=mesh['fsdp'=32,'tp'=8] {'tp'}, dimensions={4}, use_global_device_ids=true | all-gather | bytes 589824 | tf_op jit(solution)/shard_map/all_gather | solution.py:105
  310.2 25.4 %all-gather.1 = bf16[1,1,4,32,8,256]{5,3,4,2,1,0:T(8,128)(2,1)S(1)} all-gather(bf16[1,1,4,32,1,256]{5,3,4,2,1,0:T(8,128)(2,1)S(1)} %bitcast.216), channel_id=3, replica_groups=mesh['fsdp'=32,'tp'=8] {'tp'}, dimensions={4}, use_global_device_ids=true | all-gather | bytes 589824 | tf_op jit(solution)/shard_map/all_gather | solution.py:105
  351.0 2.2 convert_bitcast_fusion
  354.3 3.7 %pad_maximum_fusion = bf16[2,4,896,512]{3,2,1,0:T(8,128)(2,1)} fusion(bf16[1,4,896,512]{3,2,1,0:T(8,128)(2,1)S(1)} %convert_bitcast_fusion, bf16[1,4,896,512]{3,2,1,0:T(8,128)(2,1)S(1)} %convert_bitcast_fusion.1), kind=kLoop, calls=%fused_computation.14 | loop fusion | flops 3670016 | bytes 14680064 | tf_op jit(solution)/shard_map/concatenate | solution.py:134
  (134 shorter events, 53.4 us)
Async XLA Ops:
  0.6 65.3 %copy-start = (s32[32,8]{0,1:T(8,128)S(1)}, s32[32,8]{0,1:T(8,128)}, u32[]{:S(2)}) copy-start(s32[32,8]{0,1:T(8,128)} %param.19) | copy-start | bytes 3076
  35.2 20.4 %all-to-all-start.8 = ((bf16[1,32,4,1,256]{4,2,3,0,1:T(4,128)(2,1)}), bf16[1,32,4,1,256]{4,2,3,0,1:T(4,128)(2,1)S(1)}, u32[]{:S(2)}, u32[]{:S(2)}) async-start(bf16[1,32,4,1,256]{4,2,3,0,1:T(4,128)(2,1)} %bitcast.57), calls=%async_computation.8 | async-start | bytes 131072 | tf_op jit(solution)/shard_map/all_to_all | solution.py:77
  55.6 13.1 %all-to-all-start.2 = ((bf16[1,32,4,1,256]{4,2,3,0,1:T(4,128)(2,1)}), bf16[1,32,4,1,256]{4,2,3,0,1:T(4,128)(2,1)S(1)}, u32[]{:S(2)}, u32[]{:S(2)}) async-start(bf16[1,32,4,1,256]{4,2,3,0,1:T(4,128)(2,1)} %bitcast.18), calls=%async_computation.2 | async-start | bytes 131072 | tf_op jit(solution)/shard_map/all_to_all | solution.py:77
  68.7 12.2 %all-to-all-start = ((bf16[1,32,4,1,768]{4,2,3,0,1:T(4,128)(2,1)}), bf16[1,32,4,1,768]{4,2,3,0,1:T(4,128)(2,1)S(1)}, u32[]{:S(2)}, u32[]{:S(2)}) async-start(bf16[1,32,4,1,768]{4,2,3,0,1:T(4,128)(2,1)} %bitcast.6), calls=%async_computation | async-start | bytes 393216 | tf_op jit(solution)/shard_map/all_to_all | solution.py:77
  74.3 41.2 %copy-start.8 = (pred[8]{0:T(512)(128)(4,1)}, pred[8]{0:T(512)(128)(4,1)S(1)}, u32[]{:S(2)}) copy-start(pred[8]{0:T(512)(128)(4,1)S(1)} %compare_and_fusion) | copy-start | bytes 28
  80.9 12.0 %all-to-all-start.3 = ((bf16[1,32,4,1,768]{4,2,3,0,1:T(4,128)(2,1)}), bf16[1,32,4,1,768]{4,2,3,0,1:T(4,128)(2,1)S(1)}, u32[]{:S(2)}, u32[]{:S(2)}) async-start(bf16[1,32,4,1,768]{4,2,3,0,1:T(4,128)(2,1)} %bitcast.28), calls=%async_computation.3 | async-start | bytes 393216 | tf_op jit(solution)/shard_map/all_to_all | solution.py:77
  92.9 11.2 %all-to-all-start.12 = ((bf16[1,32,4,1,256]{4,2,3,0,1:T(4,128)(2,1)}), bf16[1,32,4,1,256]{4,2,3,0,1:T(4,128)(2,1)S(1)}, u32[]{:S(2)}, u32[]{:S(2)}) async-start(bf16[1,32,4,1,256]{4,2,3,0,1:T(4,128)(2,1)} %bitcast.75), calls=%async_computation.12 | async-start | bytes 131072 | tf_op jit(solution)/shard_map/all_to_all | solution.py:77
  104.1 21.8 %copy-start.4 = (bf16[1,32,4,1,256]{4,2,3,0,1:T(4,128)(2,1)}, bf16[1,32,4,1,256]{4,2,3,0,1:T(4,128)(2,1)S(1)}, u32[]{:S(2)}) copy-start(bf16[1,32,4,1,256]{4,2,3,0,1:T(4,128)(2,1)S(1)} %all-to-all-done.12) | copy-start | bytes 196612
  104.1 11.3 %all-to-all-start.5 = ((bf16[1,32,4,1,256]{4,2,3,0,1:T(4,128)(2,1)}), bf16[1,32,4,1,256]{4,2,3,0,1:T(4,128)(2,1)S(1)}, u32[]{:S(2)}, u32[]{:S(2)}) async-start(bf16[1,32,4,1,256]{4,2,3,0,1:T(4,128)(2,1)} %bitcast.40), calls=%async_computation.5 | async-start | bytes 131072 | tf_op jit(solution)/shard_map/all_to_all | solution.py:77
  115.5 10.5 %copy-start.2 = (bf16[1,32,4,1,256]{4,2,3,0,1:T(4,128)(2,1)}, bf16[1,32,4,1,256]{4,2,3,0,1:T(4,128)(2,1)S(1)}, u32[]{:S(2)}) copy-start(bf16[1,32,4,1,256]{4,2,3,0,1:T(4,128)(2,1)S(1)} %all-to-all-done.5) | copy-start | bytes 196612
  115.5 18.0 %all-to-all-start.1 = ((bf16[1,4,8,4,1,768]{5,3,1,4,0,2:T(4,128)(2,1)}), bf16[1,4,8,4,1,768]{5,3,1,4,0,2:T(4,128)(2,1)}, u32[]{:S(2)}, u32[]{:S(2)}) async-start(bf16[1,4,8,4,1,768]{5,3,1,4,0,2:T(4,128)(2,1)} %get-tuple-element.46), calls=%async_computation.1 | async-start | bytes 393216 | tf_op jit(solution)/shard_map/all_to_all | solution.py:97
  133.4 13.9 %all-to-all-start.4 = ((bf16[1,4,8,4,1,768]{5,3,1,4,0,2:T(4,128)(2,1)}), bf16[1,4,8,4,1,768]{5,3,1,4,0,2:T(4,128)(2,1)S(1)}, u32[]{:S(2)}, u32[]{:S(2)}) async-start(bf16[1,4,8,4,1,768]{5,3,1,4,0,2:T(4,128)(2,1)} %get-tuple-element.47), calls=%async_computation.4 | async-start | bytes 393216 | tf_op jit(solution)/shard_map/all_to_all | solution.py:97
  139.6 13.4 %copy-start.6 = (s32[1,1792,1]{1,2,0:T(1,128)S(1)}, s32[1,1792,1]{1,2,0:T(1,128)}, u32[]{:S(2)}) copy-start(s32[1,1792,1]{1,2,0:T(1,128)} %get-tuple-element.35) | copy-start | bytes 21508
  147.4 19.0 %all-to-all-start.6 = ((bf16[1,32,4,1,3584]{4,2,3,0,1:T(4,128)(2,1)}), bf16[1,32,4,1,3584]{4,2,3,0,1:T(4,128)(2,1)S(1)}, u32[]{:S(2)}, u32[]{:S(2)}) async-start(bf16[1,32,4,1,3584]{4,2,3,0,1:T(4,128)(2,1)} %bitcast.45), calls=%async_computation.6 | async-start | bytes 1835008 | tf_op jit(solution)/shard_map/all_to_all | solution.py:77
  153.1 5.5 %copy-start.7 = (pred[1792]{0:T(1024)(128)(4,1)S(1)}, pred[1792]{0:T(1024)(128)(4,1)}, u32[]{:S(2)}) copy-start(pred[1792]{0:T(1024)(128)(4,1)} %get-tuple-element.34) | copy-start | bytes 5380
  166.4 26.2 %copy-start.5 = (bf16[1,32,4,1,256]{4,2,3,0,1:T(4,128)(2,1)S(1)}, bf16[1,32,4,1,256]{4,2,3,0,1:T(4,128)(2,1)}, u32[]{:S(2)}) copy-start(bf16[1,32,4,1,256]{4,2,3,0,1:T(4,128)(2,1)} %copy-done.4) | copy-start | bytes 196612
  166.4 19.9 %all-to-all-start.10 = ((bf16[1,32,4,1,3584]{4,2,3,0,1:T(4,128)(2,1)}), bf16[1,32,4,1,3584]{4,2,3,0,1:T(4,128)(2,1)S(1)}, u32[]{:S(2)}, u32[]{:S(2)}) async-start(bf16[1,32,4,1,3584]{4,2,3,0,1:T(4,128)(2,1)} %bitcast.63), calls=%async_computation.10 | async-start | bytes 1835008 | tf_op jit(solution)/shard_map/all_to_all | solution.py:77
  187.1 22.7 %all-to-all-start.9 = ((bf16[1,4,32,8,256]{4,2,1,0,3:T(8,128)(2,1)}), bf16[1,4,32,8,256]{4,2,1,0,3:T(8,128)(2,1)}, u32[]{:S(2)}, u32[]{:S(2)}) async-start(bf16[1,4,32,8,256]{4,2,1,0,3:T(8,128)(2,1)} %tile.17), calls=%async_computation.9 | async-start | bytes 1048576 | tf_op jit(solution)/shard_map/all_to_all | solution.py:18
  194.7 21.8 %copy-start.9 = (pred[8]{0:T(512)(128)(4,1)S(1)}, pred[8]{0:T(512)(128)(4,1)}, u32[]{:S(2)}) copy-start(pred[8]{0:T(512)(128)(4,1)} %copy-done.8) | copy-start | bytes 28
  210.7 22.5 %all-to-all-start.13 = ((bf16[1,4,32,8,256]{4,2,1,0,3:T(8,128)(2,1)}), bf16[1,4,32,8,256]{4,2,1,0,3:T(8,128)(2,1)}, u32[]{:S(2)}, u32[]{:S(2)}) async-start(bf16[1,4,32,8,256]{4,2,1,0,3:T(8,128)(2,1)} %tile.19), calls=%async_computation.13 | async-start | bytes 1048576 | tf_op jit(solution)/shard_map/all_to_all | solution.py:18
  262.2 87.1 %all-to-all-start.11 = ((bf16[1,4,8,4,1,3584]{5,3,1,4,0,2:T(4,128)(2,1)}), bf16[1,4,8,4,1,3584]{5,3,1,4,0,2:T(4,128)(2,1)S(1)}, u32[]{:S(2)}, u32[]{:S(2)}) async-start(bf16[1,4,8,4,1,3584]{5,3,1,4,0,2:T(4,128)(2,1)} %get-tuple-element.45), calls=%async_computation.11 | async-start | bytes 1835008 | tf_op jit(solution)/shard_map/all_to_all | solution.py:100
  267.1 43.1 %copy-start.3 = (bf16[1,32,4,1,256]{4,2,3,0,1:T(4,128)(2,1)S(1)}, bf16[1,32,4,1,256]{4,2,3,0,1:T(4,128)(2,1)}, u32[]{:S(2)}) copy-start(bf16[1,32,4,1,256]{4,2,3,0,1:T(4,128)(2,1)} %copy-done.2) | copy-start | bytes 196612
  351.0 2.2 copy-start.1
